TPU v7x, 32 devices: a whole 2x2x4 slice. The times are simulated.
32 devices in a mesh: wide: 16 (over z, y, x), narrow: 2 (over core).
Axes of the slice: x: 2, y: 2, z: 4, core: 2. Of those that a mesh axis runs over, the one named last changes fastest.
Arguments:
- pool_tokens: bfloat16 [12288, 2048], P(('wide', 'narrow')), may hold values from -6 to 6
- cotangent: bfloat16 [24576, 2048], P(('wide', 'narrow')), may hold values from -6 to 6
- slot_weights: bfloat16 [32, 3, 2048, 512], P(('wide', 'narrow')), may hold values from -6 to 6
- row_index: int32 [32, 768], P(('wide', 'narrow')), may hold values from 0 to 383
- route_weight: float32 [32, 768], P(('wide', 'narrow')), may hold values from 0.05 to 1
- slot_expert: int32 [32, 1], replicated, may hold values from 0 to 7
- next_expert: int32 [32, 1], replicated, may hold values from 0 to 7
- master: float32 [8, 3, 2048, 512], P(None, None, ('wide', 'narrow')), may hold values from -6 to 6
- moment_m: float32 [8, 3, 2048, 512], P(None, None, ('wide', 'narrow')), may hold values from -4 to 4
- moment_v: float32 [8, 3, 2048, 512], P(None, None, ('wide', 'narrow')), may hold values from 0.05 to 1
Outputs:
- token_grads: bfloat16 [12288, 2048], P(('wide', 'narrow'))
- master_next: float32 [8, 3, 2048, 512], P(None, None, ('wide', 'narrow'))
- moment_m_next: float32 [8, 3, 2048, 512], P(None, None, ('wide', 'narrow'))
- moment_v_next: float32 [8, 3, 2048, 512], P(None, None, ('wide', 'narrow'))
- next_weights: bfloat16 [32, 3, 2048, 512], P(('wide', 'narrow'))
Inputs may be any that keep to these rules, and one draw needn't show every extreme that they name: `slot_expert`: every one of the 8 experts is held by at least one slot; counts are uneven. `next_expert`: every one of the 8 experts is held by at least one slot; counts are uneven. `row_index`: indices into the pool of the slot's own device; a token may appear more than once.
All inputs are finite; a program needn't handle non-finite values.
Results may differ from a plain program's by a relative error of at most 0.0065.
Values may be sent and summed in bfloat16 or wider, within the bound.
A program may use at most 128 MiB of HBM per device.

v0:
```python
import jax
import jax.numpy as jnp
from jax import lax
from jax.sharding import PartitionSpec as P

EXPERTS = 8


def inner(left, right):
    return lax.dot_general(
        left, right, (((0,), (0,)), ((), ())), preferred_element_type=jnp.float32
    )


def against(left, right):
    return lax.dot_general(
        left, right, (((1,), (1,)), ((), ())), preferred_element_type=jnp.float32
    )


def slot_pass(rows, cotangent, weights, route):
    scale_in = weights.shape[1] ** (-0.5)
    scale_out = weights.shape[2] ** (-0.5)
    gate = jnp.dot(rows, weights[0], preferred_element_type=jnp.float32) * scale_in
    upper = jnp.dot(rows, weights[1], preferred_element_type=jnp.float32) * scale_in
    sigma = jax.nn.sigmoid(gate)
    active = gate * sigma
    hidden = (active * upper).astype(jnp.bfloat16)
    scaled = (route[:, None] * cotangent.astype(jnp.float32)).astype(jnp.bfloat16)
    back = jnp.dot(scaled, weights[2], preferred_element_type=jnp.float32) * scale_out
    d_gate = (back * upper * sigma * (1.0 + gate * (1.0 - sigma))).astype(jnp.bfloat16)
    d_up = (back * active).astype(jnp.bfloat16)
    grads = jnp.stack(
        [
            inner(rows, d_gate) * scale_in,
            inner(rows, d_up) * scale_in,
            inner(scaled, hidden) * scale_out,
        ]
    )
    inputs = (against(d_gate, weights[0]) + against(d_up, weights[1])) * scale_in
    return (grads, inputs)


def adam_step(grad, master, moment_m, moment_v):
    first = 0.9 * moment_m + 0.1 * grad
    second = 0.95 * moment_v + 0.05 * grad * grad
    fresh = master - 0.05 * (first / (jnp.sqrt(second) + 1e-08) + 0.1 * master)
    return (fresh, first, second)


def local(
    pool_tokens,
    cotangent,
    slot_weights,
    row_index,
    route_weight,
    slot_expert,
    next_expert,
    master,
    moment_m,
    moment_v,
):
    picked = row_index[0]
    rows = jnp.take(pool_tokens, picked, axis=0)
    grads, inputs = slot_pass(rows, cotangent, slot_weights[0], route_weight[0])
    token_grads = (
        jnp.zeros(pool_tokens.shape, jnp.float32).at[picked].add(inputs).astype(jnp.bfloat16)
    )
    wide_count = lax.axis_size("wide")
    narrow_count = lax.axis_size("narrow")
    members = wide_count * narrow_count
    parts, width, hidden_units = grads.shape
    block = width // members
    received = lax.all_to_all(grads, ("wide", "narrow"), split_axis=1, concat_axis=0, tiled=True)
    received = received.reshape(members, parts, block, hidden_units)
    owners = (slot_expert[:, 0][None, :] == jnp.arange(EXPERTS, dtype=jnp.int32)[:, None]).astype(
        jnp.float32
    )
    summed = jnp.einsum("es,skrh->ekrh", owners, received, precision=lax.Precision.HIGHEST)
    fresh, first, second = adam_step(summed, master, moment_m, moment_v)
    reordered = jnp.transpose(fresh.astype(jnp.bfloat16), (1, 0, 2, 3))
    outgoing = jnp.take(reordered, next_expert[:, 0], axis=1)
    arrived = lax.all_to_all(outgoing, ("wide", "narrow"), split_axis=1, concat_axis=2, tiled=True)
    next_weights = arrived.reshape(1, parts, width, hidden_units)
    return (token_grads, fresh, first, second, next_weights)


def solution(mesh):
    in_specs = (
        P(("wide", "narrow"), None),
        P(("wide", "narrow"), None),
        P(("wide", "narrow"), None, None, None),
        P(("wide", "narrow"), None),
        P(("wide", "narrow"), None),
        P(),
        P(),
        P(None, None, ("wide", "narrow"), None),
        P(None, None, ("wide", "narrow"), None),
        P(None, None, ("wide", "narrow"), None),
    )
    out_specs = (
        P(("wide", "narrow"), None),
        P(None, None, ("wide", "narrow"), None),
        P(None, None, ("wide", "narrow"), None),
        P(None, None, ("wide", "narrow"), None),
        P(("wide", "narrow"), None, None, None),
    )
    return jax.shard_map(local, mesh=mesh, in_specs=in_specs, out_specs=out_specs, check_vma=False)
```

profile of v0, /device:TPU:0, one launch (start us, length us, event | category | flops | bytes accessed | tf_op | source)
XLA Modules:
  0.0 623.8 jit_solution(776716893748135336)
XLA Ops:
  2.2 4.2 gather_fusion
  6.4 5.7 fusion.32
  12.1 4.6 fusion.29
  16.7 5.9 multiply_convert_fusion.2
  22.7 2.2 multiply_bitcast_fusion
  24.9 2.0 multiply_bitcast_fusion.1
  26.9 2.0 multiply_bitcast_fusion.2
  28.9 1.9 pad_maximum_fusion
  30.8 25.5 %copy.44 = f32[3,2048,512]{2,0,1:T(4,128)} copy(f32[3,2048,512]{2,1,0:T(8,128)S(1)} %pad_maximum_fusion) | data formatting | bytes 25165824 | tf_op jit(solution)/shard_map/stack | solution.py:33
  56.3 7.5 %all-to-all-start = ((f32[3,2048,512]{2,0,1:T(4,128)}), f32[3,2048,512]{2,0,1:T(4,128)}, u32[]{:S(2)}, u32[]{:S(2)}) async-start(f32[3,2048,512]{2,0,1:T(4,128)} %copy.44), calls=%async_computation | async-start | bytes 33554432 | tf_op jit(solution)/shard_map/all_to_all | solution.py:74
  63.9 372.5 %all-to-all-done = f32[3,2048,512]{2,0,1:T(4,128)} async-done(((f32[3,2048,512]{2,0,1:T(4,128)}), f32[3,2048,512]{2,0,1:T(4,128)}, u32[]{:S(2)}, u32[]{:S(2)}) %all-to-all-start) | async-done | bytes 12582944 | tf_op jit(solution)/shard_map/all_to_all | solution.py:74
  436.4 26.7 %convert_bitcast_fusion = (bf16[3,8,64,512]{3,1,2,0:T(8,128)(2,1)S(1)}, f32[8,3,64,512]{3,0,2,1:T(8,128)}, f32[8,3,64,512]{3,0,2,1:T(8,128)}, f32[8,3,64,512]{3,0,2,1:T(8,128)}) fusion(f32[8,3,64,512]{3,2,1,0:T(8,128)} %param.17, f32[8,3,64,512]{3,2,1,0:T(8,128)} %param.19, f32[8,3,64,512]{3,2,1,0:T(8,128)} %param.18, f32[3,32,64,512]{3,0,2,1:T(4,128)} %bitcast.10, ...), kind=kOutput, calls=%fused_computation.38 | convolution fusion | flops 313000192 | bytes 33030272 | tf_op jit(solution)/shard_map/es,skrh->ekrh/dot_general | solution.py:79
  463.6 3.7 gather_fusion.1
  467.2 6.1 select_bitcast_fusion
  473.3 3.8 all-to-all-start.1
  477.1 6.1 fusion.9
  483.3 6.0 fusion.13
  489.3 18.8 %scatter_custom_fusion = f32[384,2048]{1,0:T(8,128)} fusion(s32[768]{0:T(1024)S(1)} %fusion.38, f32[768,2048]{1,0:T(8,128)} %fusion.9, f32[768,2048]{1,0:T(8,128)} %fusion.13, f32[]{:T(128)} %constant.13.clone.1, f32[]{:T(128)} %constant.15.clone.1), kind=kCustom, calls=%fused_computation.8 | custom fusion | flops 4718592 | bytes 15728648 | tf_op jit(solution)/shard_map/scatter-add | solution.py:67
  508.1 3.4 convert_element_type.26
  511.5 3.5 copy.52
  515.0 3.5 copy.53
  518.5 3.5 copy.54
  522.0 94.9 %all-to-all-done.1 = bf16[3,32,64,512]{3,2,0,1:T(8,128)(2,1)} async-done(((bf16[3,32,64,512]{3,2,0,1:T(8,128)(2,1)}), bf16[3,32,64,512]{3,2,0,1:T(8,128)(2,1)}, u32[]{:S(2)}, u32[]{:S(2)}) %all-to-all-start.1) | async-done | bytes 6291488 | tf_op jit(solution)/shard_map/all_to_all | solution.py:83
  616.9 6.4 %copy.51 = bf16[3,32,64,512]{3,2,1,0:T(8,128)(2,1)} copy(bf16[3,32,64,512]{3,2,0,1:T(8,128)(2,1)} %all-to-all-done.1) | data formatting | bytes 12582912 | tf_op jit(solution)/shard_map/all_to_all | solution.py:83
  (35 shorter events, 2.1 us)
Async XLA Ops:
  0.6 1.6 copy-start
  6.4 5.7 copy-start.5
  12.1 4.6 copy-start.7
  16.7 6.0 copy-start.9
  16.7 6.0 copy-start.11
  16.7 6.0 copy-start.12
  22.7 2.2 copy-start.6
  56.3 7.5 %copy-start.10 = (s32[32,1]{0,1:T(1,128)S(1)}, s32[32,1]{0,1:T(1,128)}, u32[]{:S(2)}) copy-start(s32[32,1]{0,1:T(1,128)} %param.16) | copy-start | bytes 388
  56.3 380.1 %copy-start.8 = (s32[32,1]{0,1:T(1,128)S(1)}, s32[32,1]{0,1:T(1,128)}, u32[]{:S(2)}) copy-start(s32[32,1]{0,1:T(1,128)} %param.15) | copy-start | bytes 388
  56.3 380.1 %all-to-all-start = ((f32[3,2048,512]{2,0,1:T(4,128)}), f32[3,2048,512]{2,0,1:T(4,128)}, u32[]{:S(2)}, u32[]{:S(2)}) async-start(f32[3,2048,512]{2,0,1:T(4,128)} %copy.44), calls=%async_computation | async-start | bytes 33554432 | tf_op jit(solution)/shard_map/all_to_all | solution.py:74
  473.3 143.6 %all-to-all-start.1 = ((bf16[3,32,64,512]{3,2,0,1:T(8,128)(2,1)}), bf16[3,32,64,512]{3,2,0,1:T(8,128)(2,1)}, u32[]{:S(2)}, u32[]{:S(2)}) async-start(bf16[3,32,64,512]{3,2,0,1:T(8,128)(2,1)} %select_bitcast_fusion), calls=%async_computation.1 | async-start | bytes 12582912 | tf_op jit(solution)/shard_map/all_to_all | solution.py:83
  508.1 3.4 copy-start.4
  511.5 3.5 copy-start.3
  515.0 3.5 copy-start.2
  616.9 6.4 %copy-start.1 = (bf16[384,2048]{1,0:T(8,128)(2,1)S(1)}, bf16[384,2048]{1,0:T(8,128)(2,1)}, u32[]{:S(2)}) copy-start(bf16[384,2048]{1,0:T(8,128)(2,1)} %param.10) | copy-start | bytes 4718596
where the time goes:
time: 632 us; the launch traced here: 624 us
  waiting for transfers between devices  467 us (74%)
  matrix products  61.1 us (10%)
  local copies, waits for them, and re-layouts  50.9 us (8%)
  other arithmetic  31.8 us (5%)
  starting transfers between devices  11.3 us (2%)
    all_to_all x1, waiting for transfers between devices, local(): lax.all_to_all(grads, ('wide', 'narrow'), split_axis=1, concat_axis=0, ti...  373 us
    all_to_all x1, waiting for transfers between devices, local(): lax.all_to_all(outgoing, ('wide', 'narrow'), split_axis=1, concat_axis=2,...  94.9 us
    dot_general x1, matrix products, local(): jnp.einsum('es,skrh->ekrh', owners, received, precision=lax.Precision.HIG...  26.7 us
    another operation x1, local copies, waits for them, and re-layouts, slot_pass(): jnp.stack([inner(rows, d_gate) * scale_in, inner(rows, d_up) * scale_in,...  25.5 us
    scatter-add x1, other arithmetic, local(): jnp.zeros(pool_tokens.shape, jnp.float32).at[picked].add(inputs)  18.8 us
  transfers between devices with their start and end apart: 2, of which 2 were waited for; matrix products, arithmetic and copies ran while one was open for 7% of the time, Pallas kernels for 0%

commit v1 on v0

--- a/solution.py
+++ b/solution.py
@@ -80,7 +80,15 @@
     fresh, first, second = adam_step(summed, master, moment_m, moment_v)
     reordered = jnp.transpose(fresh.astype(jnp.bfloat16), (1, 0, 2, 3))
     outgoing = jnp.take(reordered, next_expert[:, 0], axis=1)
-    arrived = lax.all_to_all(outgoing, ("wide", "narrow"), split_axis=1, concat_axis=2, tiled=True)
+    arrived = jnp.concatenate(
+        lax.all_to_all(
+            jnp.stack(jnp.split(outgoing, lax.axis_size(("wide", "narrow")), axis=1)),
+            ("wide", "narrow"),
+            0,
+            0,
+        ),
+        axis=2,
+    )
     next_weights = arrived.reshape(1, parts, width, hidden_units)
     return (token_grads, fresh, first, second, next_weights)
 

time: 632 us -> 653 us (1.033)
  local copies, waits for them, and re-layouts: 50.9 us -> 75 us
    unnamed x29 -> x58, local copies, waits for them, and re-layouts: 10.5 us -> 33.9 us
where the time goes in v1:
time: 653 us; the launch traced here: 644 us
  waiting for transfers between devices  465 us (71%)
  local copies, waits for them, and re-layouts  75 us (11%)
  matrix products  61.3 us (9%)
  other arithmetic  29.8 us (5%)
  starting transfers between devices  11.1 us (2%)
    all_to_all x1, waiting for transfers between devices, local(): lax.all_to_all(grads, ('wide', 'narrow'), split_axis=1, concat_axis=0, ti...  373 us
    all_to_all x1, waiting for transfers between devices, local(): lax.all_to_all(jnp.stack(jnp.split(outgoing, lax.axis_size(('wide', 'narr...  92.9 us
    unnamed x58, local copies, waits for them, and re-layouts  33.9 us
    dot_general x1, matrix products, local(): jnp.einsum('es,skrh->ekrh', owners, received, precision=lax.Precision.HIG...  26.9 us
    another operation x1, local copies, waits for them, and re-layouts, slot_pass(): jnp.stack([inner(rows, d_gate) * scale_in, inner(rows, d_up) * scale_in,...  25.5 us
    scatter-add x1, other arithmetic, local(): jnp.zeros(pool_tokens.shape, jnp.float32).at[picked].add(inputs)  18.8 us
  transfers between devices with their start and end apart: 2, of which 2 were waited for; matrix products, arithmetic and copies ran while one was open for 7% of the time, Pallas kernels for 0%

profile of v1, /device:TPU:0, one launch (start us, length us, event | category | flops | bytes accessed | tf_op | source)
XLA Modules:
  0.0 643.9 jit_solution(6053165971065901674)
XLA Ops:
  2.9 4.2 gather_fusion
  7.1 5.7 fusion.32
  12.8 4.6 fusion.29
  17.4 5.9 multiply_convert_fusion.2
  23.4 2.2 multiply_bitcast_fusion
  25.6 2.0 multiply_bitcast_fusion.1
  27.6 2.0 multiply_bitcast_fusion.2
  29.6 1.9 pad_maximum_fusion
  31.5 25.5 %copy.75 = f32[3,2048,512]{2,0,1:T(4,128)} copy(f32[3,2048,512]{2,1,0:T(8,128)S(1)} %pad_maximum_fusion) | data formatting | bytes 25165824 | tf_op jit(solution)/shard_map/stack | solution.py:33
  57.0 7.5 %all-to-all-start = ((f32[3,2048,512]{2,0,1:T(4,128)}), f32[3,2048,512]{2,0,1:T(4,128)}, u32[]{:S(2)}, u32[]{:S(2)}) async-start(f32[3,2048,512]{2,0,1:T(4,128)} %copy.75), calls=%async_computation | async-start | bytes 33554432 | tf_op jit(solution)/shard_map/all_to_all | solution.py:74
  64.5 372.6 %all-to-all-done = f32[3,2048,512]{2,0,1:T(4,128)} async-done(((f32[3,2048,512]{2,0,1:T(4,128)}), f32[3,2048,512]{2,0,1:T(4,128)}, u32[]{:S(2)}, u32[]{:S(2)}) %all-to-all-start) | async-done | bytes 12582944 | tf_op jit(solution)/shard_map/all_to_all | solution.py:74
  437.1 26.9 %convert_bitcast_fusion = (bf16[3,8,64,512]{3,1,2,0:T(8,128)(2,1)S(1)}, f32[8,3,64,512]{3,0,2,1:T(8,128)}, f32[8,3,64,512]{3,0,2,1:T(8,128)}, f32[8,3,64,512]{3,0,2,1:T(8,128)}) fusion(f32[8,3,64,512]{3,2,1,0:T(8,128)} %param.17, f32[8,3,64,512]{3,2,1,0:T(8,128)} %param.19, f32[8,3,64,512]{3,2,1,0:T(8,128)} %param.18, f32[3,32,64,512]{3,0,2,1:T(4,128)} %bitcast.10, ...), kind=kOutput, calls=%fused_computation.38 | convolution fusion | flops 313000192 | bytes 33030272 | tf_op jit(solution)/shard_map/es,skrh->ekrh/dot_general | solution.py:79
  464.4 3.7 gather_fusion.1
  468.1 3.4 select_bitcast_fusion
  493.6 3.6 all-to-all-start.1
  497.2 6.1 fusion.9
  503.4 6.0 fusion.13
  509.4 18.8 %scatter_custom_fusion = f32[384,2048]{1,0:T(8,128)} fusion(s32[768]{0:T(1024)S(1)} %fusion.70, f32[768,2048]{1,0:T(8,128)} %fusion.9, f32[768,2048]{1,0:T(8,128)} %fusion.13, f32[]{:T(128)} %constant.13.clone.1, f32[]{:T(128)} %constant.15.clone.1), kind=kCustom, calls=%fused_computation.8 | custom fusion | flops 4718592 | bytes 15728648 | tf_op jit(solution)/shard_map/scatter-add | solution.py:67
  528.2 3.4 convert_element_type.26
  531.6 5.5 copy.83
  537.2 3.5 copy.84
  540.7 3.5 copy.85
  544.1 92.9 %all-to-all-done.1 = bf16[32,3,1,64,512]{4,3,1,2,0:T(8,128)(2,1)} async-done(((bf16[32,3,1,64,512]{4,3,1,2,0:T(8,128)(2,1)}), bf16[32,3,1,64,512]{4,3,1,2,0:T(8,128)(2,1)}, u32[]{:S(2)}, u32[]{:S(2)}) %all-to-all-start.1) | async-done | bytes 6291488 | tf_op jit(solution)/shard_map/all_to_all | solution.py:84
  637.0 6.4 copy.82
  (64 shorter events, 24.9 us)
Async XLA Ops:
  0.6 2.2 copy-start
  7.1 5.7 copy-start.4
  12.8 4.6 copy-start.6
  17.4 6.0 copy-start.8
  17.4 6.0 copy-start.10
  17.4 6.0 copy-start.11
  23.4 2.2 copy-start.5
  57.0 7.5 %copy-start.9 = (s32[32,1]{0,1:T(1,128)S(1)}, s32[32,1]{0,1:T(1,128)}, u32[]{:S(2)}) copy-start(s32[32,1]{0,1:T(1,128)} %param.16) | copy-start | bytes 388
  57.0 380.1 %copy-start.7 = (s32[32,1]{0,1:T(1,128)S(1)}, s32[32,1]{0,1:T(1,128)}, u32[]{:S(2)}) copy-start(s32[32,1]{0,1:T(1,128)} %param.15) | copy-start | bytes 388
  57.0 380.1 %all-to-all-start = ((f32[3,2048,512]{2,0,1:T(4,128)}), f32[3,2048,512]{2,0,1:T(4,128)}, u32[]{:S(2)}, u32[]{:S(2)}) async-start(f32[3,2048,512]{2,0,1:T(4,128)} %copy.75), calls=%async_computation | async-start | bytes 33554432 | tf_op jit(solution)/shard_map/all_to_all | solution.py:74
  493.6 143.4 %all-to-all-start.1 = ((bf16[32,3,1,64,512]{4,3,1,2,0:T(8,128)(2,1)}), bf16[32,3,1,64,512]{4,3,1,2,0:T(8,128)(2,1)}, u32[]{:S(2)}, u32[]{:S(2)}) async-start(bf16[32,3,1,64,512]{4,3,1,2,0:T(8,128)(2,1)} %fusion.36), calls=%async_computation.1 | async-start | bytes 12582912 | tf_op jit(solution)/shard_map/all_to_all | solution.py:84
  528.2 9.0 %copy-start.3 = (f32[8,3,64,512]{3,0,2,1:T(8,128)S(1)}, f32[8,3,64,512]{3,0,2,1:T(8,128)}, u32[]{:S(2)}) copy-start(f32[8,3,64,512]{3,0,2,1:T(8,128)} %get-tuple-element.28) | copy-start | bytes 9437188
  531.6 9.0 %copy-start.2 = (f32[8,3,64,512]{3,0,2,1:T(8,128)S(1)}, f32[8,3,64,512]{3,0,2,1:T(8,128)}, u32[]{:S(2)}) copy-start(f32[8,3,64,512]{3,0,2,1:T(8,128)} %get-tuple-element.27) | copy-start | bytes 9437188
  637.0 6.4 copy-start.1
